TPU v7x, 32 devices: a whole 2x2x4 slice. The times are simulated.
32 devices in a mesh: img: 8 (over y, x, core), seq: 4 (over z).
Axes of the slice: x: 2, y: 2, z: 4, core: 2. Of those that a mesh axis runs over, the one named last changes fastest.
Arguments:
- x_big: bfloat16 [128, 200, 768], P(('img', 'seq')), may hold values from -6 to 6
- x_small: bfloat16 [512, 40, 768], P(('img', 'seq')), may hold values from -6 to 6
- mask_big: int32 [128, 200], P('img'), may hold values from 0 to 1, as said below
- mask_small: int32 [512, 40], P('img'), may hold values from 0 to 1, as said below
- ln1_gain: float32 [768], P('seq'), may hold values from 0.5 to 1.5
- ln1_bias: float32 [768], P('seq'), may hold values from -1.75 to 1.75
- w_qkv: float32 [768, 2304], P('img', 'seq'), may hold values from -0.21875 to 0.21875
- b_qv: float32 [1536], P('seq'), may hold values from -3 to 3
- w_out: float32 [768, 768], P('img', 'seq'), may hold values from -0.625 to 0.625
- b_out: float32 [768], P('seq'), may hold values from -1.75 to 1.75
- ln2_gain: float32 [768], P('seq'), may hold values from 0.5 to 1.5
- ln2_bias: float32 [768], P('seq'), may hold values from -1.75 to 1.75
- w_up: float32 [768, 3072], P('img', 'seq'), may hold values from -0.21875 to 0.21875
- b_up: float32 [3072], P('seq'), may hold values from -3 to 3
- w_down: float32 [3072, 768], P('img', 'seq'), may hold values from -0.109375 to 0.109375
- b_down: float32 [768], P('seq'), may hold values from -1.75 to 1.75
- dy_big: bfloat16 [128, 200, 768], P(('img', 'seq')), may hold values from -6 to 6
- dy_small: bfloat16 [512, 40, 768], P(('img', 'seq')), may hold values from -6 to 6
Outputs:
- y_big: bfloat16 [128, 200, 768], P(('img', 'seq'))
- y_small: bfloat16 [512, 40, 768], P(('img', 'seq'))
- dx_big: bfloat16 [128, 200, 768], P(('img', 'seq'))
- dx_small: bfloat16 [512, 40, 768], P(('img', 'seq'))
- g_ln1_gain: float32 [768], P('seq')
- g_ln1_bias: float32 [768], P('seq')
- g_w_qkv: float32 [768, 2304], P('img', 'seq')
- g_b_qv: float32 [1536], P('seq')
- g_w_out: float32 [768, 768], P('img', 'seq')
- g_b_out: float32 [768], P('seq')
- g_ln2_gain: float32 [768], P('seq')
- g_ln2_bias: float32 [768], P('seq')
- g_w_up: float32 [768, 3072], P('img', 'seq')
- g_b_up: float32 [3072], P('seq')
- g_w_down: float32 [3072, 768], P('img', 'seq')
- g_b_down: float32 [768], P('seq')
Inputs may be any that keep to these rules, and one draw needn't show every extreme that they name: `mask_big`: each 224px crop's mask is 1 on its first 175 to 200 slots and 0 after; some crop has all slots valid and some the fewest. `mask_small`: each 96px crop's mask is 1 on its first 35 to 40 slots and 0 after; some crop has all slots valid and some the fewest.
All inputs are finite; a program needn't handle non-finite values.
Results may differ from a plain program's by a relative error of at most 0.014.
Values may be sent and summed in bfloat16 or wider, within the bound.
A program may use at most 192 MiB of HBM per device.

v0:
```python
import jax
import jax.numpy as jnp
from jax import lax
from jax.sharding import PartitionSpec as P

HEADS = 12
HEAD_DIM = 64
AXES = ("img", "seq")
EPSILON = 1e-06
NEGATIVE = -1e30


def layer_norm(values, gain_vec, shift_vec):
    row_mean = jnp.mean(values, axis=-1, keepdims=True)
    centred = values - row_mean
    variance = jnp.mean(centred * centred, axis=-1, keepdims=True)
    return centred * lax.rsqrt(variance + EPSILON) * gain_vec + shift_vec


def gelu_exact(values):
    return jax.nn.gelu(values, approximate=False)


def head_scores(heads_in, key_valid):
    crop_count, length = (heads_in.shape[0], heads_in.shape[1])
    pieces = heads_in.reshape(crop_count, length, 3, HEADS, HEAD_DIM)
    queries, key_rows, value_rows = (pieces[:, :, 0], pieces[:, :, 1], pieces[:, :, 2])
    raw_scores = jnp.einsum(
        "cqhd,ckhd->chqk", queries, key_rows, preferred_element_type=jnp.float32
    )
    scores = jnp.where(key_valid[:, None, None, :] > 0, raw_scores * HEAD_DIM ** (-0.5), NEGATIVE)
    return (queries, key_rows, value_rows, scores)


def attend(heads_in, key_valid):
    crop_count, length = (heads_in.shape[0], heads_in.shape[1])
    queries, key_rows, value_rows, scores = head_scores(heads_in, key_valid)
    row_max = jnp.max(scores, axis=-1, keepdims=True)
    exponent = jnp.exp(scores - row_max)
    row_total = jnp.sum(exponent, axis=-1, keepdims=True)
    softmax_w = (exponent / row_total).astype(jnp.bfloat16)
    mixed_out = jnp.einsum(
        "chqk,ckhd->cqhd", softmax_w, value_rows, preferred_element_type=jnp.float32
    )
    log_total = row_max + jnp.log(row_total)
    return (mixed_out.astype(jnp.bfloat16).reshape(crop_count * length, -1), log_total)


def attend_back(heads_in, key_valid, log_total, grad_heads):
    crop_count, length = (heads_in.shape[0], heads_in.shape[1])
    queries, key_rows, value_rows, scores = head_scores(heads_in, key_valid)
    softmax_f = jnp.exp(scores - log_total)
    grad_mixed = grad_heads.reshape(crop_count, length, HEADS, HEAD_DIM)
    grad_soft = jnp.einsum(
        "cqhd,ckhd->chqk", grad_mixed, value_rows, preferred_element_type=jnp.float32
    )
    inner_sum = jnp.sum(softmax_f * grad_soft, axis=-1, keepdims=True)
    grad_raw = (softmax_f * (grad_soft - inner_sum) * HEAD_DIM ** (-0.5)).astype(jnp.bfloat16)
    grad_query = jnp.einsum(
        "chqk,ckhd->cqhd", grad_raw, key_rows, preferred_element_type=jnp.float32
    )
    grad_key = jnp.einsum("chqk,cqhd->ckhd", grad_raw, queries, preferred_element_type=jnp.float32)
    grad_value = jnp.einsum(
        "chqk,cqhd->ckhd",
        softmax_f.astype(jnp.bfloat16),
        grad_mixed,
        preferred_element_type=jnp.float32,
    )
    stacked = jnp.stack([grad_query, grad_key, grad_value], axis=2).astype(jnp.bfloat16)
    return stacked.reshape(crop_count * length, -1)


def gather_mats(mats):
    n_img, n_seq = (lax.axis_size("img"), lax.axis_size("seq"))
    flat = jnp.concatenate([m.astype(jnp.bfloat16).reshape(-1, 64) for m in mats], axis=0)
    whole = lax.all_gather(flat, AXES, axis=0, tiled=False)
    outs, at = ([], 0)
    for m in mats:
        rows = m.size // 64
        piece = whole[:, at : at + rows].reshape((n_img, n_seq) + m.shape)
        at += rows
        if m.ndim == 2:
            piece = piece.transpose(0, 2, 1, 3).reshape(n_img * m.shape[0], n_seq * m.shape[1])
        else:
            piece = piece[0].reshape(-1)
        outs.append(piece)
    return outs


def scatter_mats(mats):
    n_img, n_seq = (lax.axis_size("img"), lax.axis_size("seq"))
    blocks = []
    for m in mats:
        rows, cols = (m.shape[0] // n_img, m.shape[1] // n_seq)
        b = m.astype(jnp.bfloat16).reshape(n_img, rows, n_seq, cols).transpose(0, 2, 1, 3)
        blocks.append(b.reshape(n_img * n_seq, -1, 128))
    flat = jnp.concatenate(blocks, axis=1)
    mine = lax.psum_scatter(flat, AXES, scatter_dimension=0, tiled=False)
    outs, at = ([], 0)
    for m, b in zip(mats, blocks):
        piece = mine[at : at + b.shape[1]]
        at += b.shape[1]
        outs.append(piece.reshape(m.shape[0] // n_img, m.shape[1] // n_seq).astype(jnp.float32))
    return outs


def body(
    x_big,
    x_small,
    mask_big,
    mask_small,
    ln1_gain,
    ln1_bias,
    w_qkv,
    b_qv,
    w_out,
    b_out,
    ln2_gain,
    ln2_bias,
    w_up,
    b_up,
    w_down,
    b_down,
    dy_big,
    dy_small,
):
    n_seq = lax.axis_size("seq")
    where = lax.axis_index("seq")
    model_width = x_big.shape[2]
    big_crops, big_length = (x_big.shape[0], x_big.shape[1])
    small_crops, small_length = (x_small.shape[0], x_small.shape[1])
    big_rows = big_crops * big_length
    mask_big = lax.dynamic_slice_in_dim(mask_big, where * big_crops, big_crops, 0)
    mask_small = lax.dynamic_slice_in_dim(mask_small, where * small_crops, small_crops, 0)
    qkv_full, gain_one, shift_one, bias_qv, bias_out, gain_two, shift_two, bias_up, bias_down = (
        gather_mats([w_qkv, ln1_gain, ln1_bias, b_qv, b_out, ln2_gain, ln2_bias, b_up, b_down])
    )
    out_full, up_full, down_full = gather_mats([w_out, w_up, w_down])
    gain_one, shift_one, bias_qv, bias_out, gain_two, shift_two, bias_up, bias_down = tuple(
        (
            vec.astype(jnp.float32)
            for vec in (
                gain_one,
                shift_one,
                bias_qv,
                bias_out,
                gain_two,
                shift_two,
                bias_up,
                bias_down,
            )
        )
    )
    tokens = jnp.concatenate(
        [x_big.reshape(big_rows, model_width), x_small.reshape(-1, model_width)], axis=0
    ).astype(jnp.float32)
    normed_one, pull_one = jax.vjp(layer_norm, tokens, gain_one, shift_one)
    input_one = normed_one.astype(jnp.bfloat16)
    bias_qkv = jnp.concatenate(
        [bias_qv[:model_width], jnp.zeros((model_width,), jnp.float32), bias_qv[model_width:]]
    )
    projected = (
        jnp.dot(input_one, qkv_full, preferred_element_type=jnp.float32) + bias_qkv
    ).astype(jnp.bfloat16)
    heads_big = projected[:big_rows].reshape(big_crops, big_length, -1)
    heads_small = projected[big_rows:].reshape(small_crops, small_length, -1)
    mixed_big, total_big = attend(heads_big, mask_big)
    mixed_small, total_small = attend(heads_small, mask_small)
    mixed_tok = jnp.concatenate([mixed_big, mixed_small], axis=0)
    middle = tokens + jnp.dot(mixed_tok, out_full, preferred_element_type=jnp.float32) + bias_out
    normed_two, pull_two = jax.vjp(layer_norm, middle, gain_two, shift_two)
    input_two = normed_two.astype(jnp.bfloat16)
    up_proj = jnp.dot(input_two, up_full, preferred_element_type=jnp.float32) + bias_up
    activated_f, pull_act = jax.vjp(gelu_exact, up_proj)
    activated = activated_f.astype(jnp.bfloat16)
    result = middle + jnp.dot(activated, down_full, preferred_element_type=jnp.float32) + bias_down
    grad_out = jnp.concatenate(
        [dy_big.reshape(big_rows, model_width), dy_small.reshape(-1, model_width)], axis=0
    )
    grad_down = jnp.einsum("ti,tj->ij", activated, grad_out, preferred_element_type=jnp.float32)
    grad_bias_down = jnp.sum(grad_out.astype(jnp.float32), axis=0)
    grad_act = jnp.einsum("tj,ij->ti", grad_out, down_full, preferred_element_type=jnp.float32)
    (grad_up_f,) = pull_act(grad_act)
    grad_up_b = grad_up_f.astype(jnp.bfloat16)
    grad_upw = jnp.einsum("ti,tj->ij", input_two, grad_up_b, preferred_element_type=jnp.float32)
    grad_bias_up = jnp.sum(grad_up_b.astype(jnp.float32), axis=0)
    grad_in_two = jnp.einsum("tj,ij->ti", grad_up_b, up_full, preferred_element_type=jnp.float32)
    grad_middle_ln, grad_gain_two, grad_shift_two = pull_two(grad_in_two)
    grad_middle = grad_out.astype(jnp.float32) + grad_middle_ln
    grad_branch = grad_middle.astype(jnp.bfloat16)
    grad_bias_out = jnp.sum(grad_branch.astype(jnp.float32), axis=0)
    grad_outw = jnp.einsum("ti,tj->ij", mixed_tok, grad_branch, preferred_element_type=jnp.float32)
    grad_mixed = jnp.einsum(
        "tj,ij->ti", grad_branch, out_full, preferred_element_type=jnp.float32
    ).astype(jnp.bfloat16)
    grad_projected = jnp.concatenate(
        [
            attend_back(heads_big, mask_big, total_big, grad_mixed[:big_rows]),
            attend_back(heads_small, mask_small, total_small, grad_mixed[big_rows:]),
        ],
        axis=0,
    )
    grad_qkvw = jnp.einsum(
        "ti,tj->ij", input_one, grad_projected, preferred_element_type=jnp.float32
    )
    grad_proj_sums = jnp.sum(grad_projected.astype(jnp.float32), axis=0)
    grad_bias_qv = jnp.concatenate(
        [grad_proj_sums[:model_width], grad_proj_sums[2 * model_width :]]
    )
    grad_in_one = jnp.einsum(
        "tj,ij->ti", grad_projected, qkv_full, preferred_element_type=jnp.float32
    )
    grad_tokens_ln, grad_gain_one, grad_shift_one = pull_one(grad_in_one)
    grad_tokens = (grad_middle + grad_tokens_ln).astype(jnp.bfloat16)
    vectors = (
        grad_gain_one,
        grad_shift_one,
        grad_bias_qv,
        grad_bias_out,
        grad_gain_two,
        grad_shift_two,
        grad_bias_up,
        grad_bias_down,
    )
    vector_sums = lax.psum(jnp.concatenate(vectors), AXES)
    vec_out, at = ([], 0)
    for v in vectors:
        width = v.shape[0] // n_seq
        vec_out.append(lax.dynamic_slice(vector_sums, (at + where * width,), (width,)))
        at += v.shape[0]
    g_up, g_down = scatter_mats([grad_upw, grad_down])
    g_qkv, g_out = scatter_mats([grad_qkvw, grad_outw])
    y_big = result[:big_rows].reshape(big_crops, big_length, model_width).astype(jnp.bfloat16)
    y_small = result[big_rows:].reshape(small_crops, small_length, model_width).astype(jnp.bfloat16)
    dx_big = grad_tokens[:big_rows].reshape(big_crops, big_length, model_width)
    dx_small = grad_tokens[big_rows:].reshape(small_crops, small_length, model_width)
    return (
        y_big,
        y_small,
        dx_big,
        dx_small,
        vec_out[0],
        vec_out[1],
        g_qkv,
        vec_out[2],
        g_out,
        vec_out[3],
        vec_out[4],
        vec_out[5],
        g_up,
        vec_out[6],
        g_down,
        vec_out[7],
    )


def solution(mesh):
    rows3 = P(AXES, None, None)
    placed = (
        rows3,
        rows3,
        P("img", None),
        P("img", None),
        P("seq"),
        P("seq"),
        P("img", "seq"),
        P("seq"),
        P("img", "seq"),
        P("seq"),
        P("seq"),
        P("seq"),
        P("img", "seq"),
        P("seq"),
        P("img", "seq"),
        P("seq"),
        rows3,
        rows3,
    )
    return jax.shard_map(
        body,
        mesh=mesh,
        in_specs=placed,
        out_specs=(rows3,) * 4
        + (
            P("seq"),
            P("seq"),
            P("img", "seq"),
            P("seq"),
            P("img", "seq"),
            P("seq"),
            P("seq"),
            P("seq"),
            P("img", "seq"),
            P("seq"),
            P("img", "seq"),
            P("seq"),
        ),
        check_vma=False,
    )
```

profile of v0, /device:TPU:0, one launch (start us, length us, event | category | flops | bytes accessed | tf_op | source)
XLA Modules:
  0.0 870.6 jit_solution(1051177203787296150)
XLA Ops:
  25.0 55.9 %all-gather.7.cloned.1.call-done = bf16[32,900,64]{1,2,0:T(8,128)(2,1)} async-done(((bf16[1,900,64]{1,2,0:T(8,128)(2,1)}), bf16[32,900,64]{1,2,0:T(8,128)(2,1)}) %all-gather.7.cloned.1.call-update) | async-done | bytes 3686416 | tf_op jit(solution)/shard_map/all_gather | solution.py:76
  97.2 10.8 %reshape.350 = bf16[8,4,96,576]{3,2,1,0:T(8,128)(2,1)} reshape(bf16[32,864,64]{2,1,0:T(8,128)(2,1)} %copy.143) | data formatting | bytes 7077888 | tf_op jit(solution)/shard_map/reshape | solution.py:80
  122.0 9.1 %fusion.8 = bf16[1440,2304]{1,0:T(8,128)(2,1)S(1)} fusion(bf16[768,2304]{1,0:T(8,128)(2,1)} %reshape.351, f32[2304]{0:T(1024)S(1)} %pad_maximum_fusion.12, f32[768]{0:T(1024)S(1)} %reshape.378, f32[768]{0:T(1024)S(1)} %reshape.377, f32[1440]{0:T(1024)S(1)} %fusion.103, f32[1440]{0:T(1024)S(1)} %broadcast_multiply_fusion.1, ...), kind=kOutput, calls=%fused_computation.22 | convolution fusion | flops 5112668160 | bytes 12413184 | tf_op jit(solution)/shard_map/dot_general | solution.py:163
  136.7 9.8 %reshape_reshape.9 = bf16[16,40,3,12,64]{4,3,2,1,0:T(8,128)(2,1)} reshape(bf16[640,2304]{1,0:T(8,128)(2,1)} %slice.190) | data formatting | bytes 5898240 | tf_op jit(solution)/shard_map/reshape;reshape | solution.py:26
  168.5 12.1 %reshape.398 = bf16[4,200,3,12,64]{4,3,2,1,0:T(8,128)(2,1)} reshape(bf16[800,2304]{1,0:T(8,128)(2,1)} %slice.186) | data formatting | bytes 7372800 | tf_op jit(solution)/shard_map/reshape;reshape | solution.py:26
  239.9 14.1 %fusion.135 = (bf16[32,1152,64]{1,2,0:T(8,128)(2,1)}, bf16[32,1152,64]{1,2,0:T(8,128)(2,1)}) fusion(bf16[32,2592,64]{1,2,0:T(8,128)(2,1)} %all-gather.9.cloned.1.call-done), kind=kLoop, calls=%fused_computation.187 | loop fusion | bytes 18874368 | tf_op jit(solution)/shard_map/slice | solution.py:80
  254.0 9.6 %copy.174 = bf16[32,1152,64]{2,1,0:T(8,128)(2,1)} copy(bf16[32,1152,64]{1,2,0:T(8,128)(2,1)} %get-tuple-element.77) | data formatting | bytes 9437184 | tf_op jit(solution)/shard_map/slice | solution.py:80
  263.7 15.5 %reshape.361 = bf16[8,4,384,192]{3,2,1,0:T(8,128)(2,1)} reshape(bf16[32,1152,64]{2,1,0:T(8,128)(2,1)} %copy.174) | data formatting | bytes 9437184 | tf_op jit(solution)/shard_map/reshape | solution.py:80
  293.6 9.6 %copy.170 = bf16[32,1152,64]{2,1,0:T(8,128)(2,1)} copy(bf16[32,1152,64]{1,2,0:T(8,128)(2,1)} %get-tuple-element.78) | data formatting | bytes 9437184 | tf_op jit(solution)/shard_map/slice | solution.py:80
  303.3 13.4 %reshape.359 = bf16[8,4,96,768]{3,2,1,0:T(8,128)(2,1)} reshape(bf16[32,1152,64]{2,1,0:T(8,128)(2,1)} %copy.170) | data formatting | bytes 9437184 | tf_op jit(solution)/shard_map/reshape | solution.py:80
  328.1 48.1 %multiply_convert_fusion = (bf16[1440,3072]{1,0:T(8,128)(2,1)}, f32[1440,3072]{1,0:T(8,128)}, f32[1440,3072]{1,0:T(8,128)}) fusion(f32[3072]{0:T(1024)S(1)} %reshape.382, bf16[768,3072]{1,0:T(8,128)(2,1)S(1)} %bitcast.185, f32[1440,768]{1,0:T(8,128)S(1)} %get-tuple-element.108, f32[768]{0:T(1024)S(1)} %reshape.381, f32[768]{0:T(1024)S(1)} %reshape.380, ...), kind=kOutput, calls=%fused_computation.6 | convolution fusion | flops 7092264960 | bytes 53409024 | tf_op jit(solution)/shard_map/dot_general | solution.py:173
  376.3 21.3 %convert_reduce_fusion = (f32[3072]{0:T(1024)}, bf16[1440,3072]{1,0:T(8,128)(2,1)}) fusion(f32[1440,3072]{1,0:T(8,128)} %get-tuple-element.76, bf16[3072,768]{0,1:T(8,128)(2,1)S(1)} %bitcast.184, bf16[640,768]{1,0:T(8,128)(2,1)} %bitcast.187, bf16[800,768]{1,0:T(8,128)(2,1)S(1)} %bitcast.177, f32[1440,3072]{1,0:T(8,128)} %get-tuple-element.109, ...), kind=kOutput, calls=%fused_computation.4 | convolution fusion | flops 6874395648 | bytes 51191808 | tf_op jit(solution)/shard_map/tj,ij->ti/dot_general | solution.py:182
  397.6 13.7 %multiply_reduce_fusion.1 = (f32[768]{0:T(1024)}, f32[1440]{0:T(1024)S(1)}, f32[768]{0:T(1024)}, f32[1440,768]{1,0:T(8,128)S(1)}) fusion(f32[1440,768]{1,0:T(8,128)S(1)} %get-tuple-element.108, f32[1440]{0:T(1024)S(1)} %fusion.104, f32[1440]{0:T(1024)S(1)} %broadcast_multiply_fusion, f32[768]{0:T(1024)S(1)} %reshape.380, ...), kind=kOutput, calls=%fused_computation.67 | convolution fusion | flops 6803616768 | bytes 22439808 | tf_op jit(solution)/shard_map/tj,ij->ti/dot_general | solution.py:187
  434.6 10.0 %convert_bitcast_fusion.2 = bf16[16,40,1,12,64]{4,1,3,0,2:T(8,128)(2,1)} fusion(f32[16,12,40,40]{2,3,1,0:T(8,128)} %fusion.100, f32[16,12,40,40]{2,3,1,0:T(8,128)} %copy-done.8, f32[16,12,40]{2,1,0:T(8,128)S(1)} %copy-done.35, bf16[16,40,1,12,64]{4,3,2,1,0:T(8,128)(2,1)} %copy-done.26), kind=kOutput, calls=%fused_computation.98 | convolution fusion | flops 41971240 | bytes 4454400 | tf_op jit(solution)/shard_map/chqk,ckhd->cqhd/dot_general | solution.py:59
  444.6 9.2 %convert_bitcast_fusion.1 = bf16[16,40,1,12,64]{4,1,3,0,2:T(8,128)(2,1)} fusion(f32[16,12,40,40]{2,3,1,0:T(8,128)} %fusion.100, f32[16,12,40,40]{2,3,1,0:T(8,128)} %copy-done.8, f32[16,12,40]{2,1,0:T(8,128)S(1)} %copy-done.35, bf16[16,40,1,12,64]{4,3,2,1,0:T(8,128)(2,1)S(1)} %copy-done.25), kind=kOutput, calls=%fused_computation.97 | convolution fusion | flops 41971240 | bytes 4454400 | tf_op jit(solution)/shard_map/chqk,cqhd->ckhd/dot_general | solution.py:62
  475.5 19.7 %fusion.92 = bf16[4,200,1,12,64]{1,4,3,0,2:T(8,128)(2,1)} fusion(f32[4,12,200,200]{2,3,1,0:T(8,128)} %fusion.81, f32[4,12,200]{2,1,0:T(8,128)S(1)} %copy-done.46, f32[4,12,200,200]{2,3,1,0:T(8,128)} %copy-done.3, pred[4,200]{1,0:T(4,128)(4,1)S(1)} %copy-done.52, bf16[4,200,1,12,64]{1,4,3,0,2:T(8,128)(2,1)S(1)} %copy-done.17), kind=kOutput, calls=%fused_computation.122 | convolution fusion | flops 267504192 | bytes 17856800 | tf_op jit(solution)/shard_map/chqk,ckhd->cqhd/dot_general | solution.py:59
  495.2 19.0 %fusion.87 = bf16[4,200,1,12,64]{1,4,3,0,2:T(8,128)(2,1)} fusion(f32[4,12,200,200]{2,3,1,0:T(8,128)} %fusion.81, f32[4,12,200]{2,1,0:T(8,128)S(1)} %copy-done.46, f32[4,12,200,200]{2,3,1,0:T(8,128)} %copy-done.3, pred[4,200]{1,0:T(4,128)(4,1)S(1)} %copy-done.52, bf16[4,200,1,12,64]{1,4,3,0,2:T(8,128)(2,1)S(1)} %copy-done.15), kind=kOutput, calls=%fused_computation.121 | convolution fusion | flops 267504192 | bytes 17856800 | tf_op jit(solution)/shard_map/chqk,cqhd->ckhd/dot_general | solution.py:62
  528.6 12.8 %copy.203 = bf16[16,40,3,12,64]{1,0,4,3,2:T(8,128)(2,1)} copy(bf16[16,40,3,12,64]{4,1,3,0,2:T(8,128)(2,1)} %pad_maximum_fusion.2) | data formatting | bytes 5898240 | tf_op jit(solution)/shard_map/convert_element_type | solution.py:69
  541.3 14.1 %reshape.397 = bf16[640,2304]{0,1:T(8,128)(2,1)} reshape(bf16[16,40,3,12,64]{1,0,4,3,2:T(8,128)(2,1)} %copy.203) | data formatting | bytes 5898240 | tf_op jit(solution)/shard_map/convert_element_type | solution.py:69
  564.8 9.7 %convert_element_type.280 = bf16[800,2304]{0,1:T(8,128)(2,1)} reshape(bf16[4,200,3,12,64]{1,0,4,3,2:T(4,128)(2,1)} %copy.184) | data formatting | bytes 7372800 | tf_op jit(solution)/shard_map/convert_element_type | solution.py:69
  574.5 12.6 %convolution_convert_fusion = bf16[768,2304]{1,0:T(8,128)(2,1)} fusion(bf16[640,2304]{0,1:T(8,128)(2,1)} %reshape.397, bf16[800,2304]{0,1:T(8,128)(2,1)} %convert_element_type.280, f32[768]{0:T(1024)S(1)} %copy-done.54, f32[768]{0:T(1024)S(1)} %copy-done.48, f32[1440]{0:T(1024)S(1)} %copy-done.39, f32[1440]{0:T(1024)S(1)} %copy-done.37, ...), kind=kOutput, calls=%fused_computation.48 | convolution fusion | flops 5121073152 | bytes 12403968 | tf_op jit(solution)/shard_map/ti,tj->ij/dot_general | solution.py:203
  587.1 9.1 %reshape.369 = bf16[8,96,4,576]{3,2,1,0:T(4,128)(2,1)} reshape(bf16[768,2304]{1,0:T(8,128)(2,1)} %convolution_convert_fusion) | data formatting | bytes 7077888 | tf_op jit(solution)/shard_map/reshape | solution.py:95
  614.8 12.5 %convolution_convert_fusion.1 = bf16[3072,768]{1,0:T(8,128)(2,1)} fusion(bf16[1440,3072]{1,0:T(8,128)(2,1)} %get-tuple-element.75, bf16[640,768]{1,0:T(8,128)(2,1)} %bitcast.188, bf16[800,768]{1,0:T(8,128)(2,1)S(1)} %bitcast.179), kind=kOutput, calls=%fused_computation.49 | convolution fusion | flops 6801555456 | bytes 15777792 | tf_op jit(solution)/shard_map/ti,tj->ij/dot_general | solution.py:180
  639.7 14.1 %convolution_convert_fusion.2 = bf16[768,3072]{1,0:T(8,128)(2,1)} fusion(bf16[1440,3072]{1,0:T(8,128)(2,1)} %get-tuple-element.113, f32[1440,768]{1,0:T(8,128)} %copy-done.6, f32[768]{0:T(1024)S(1)} %copy-done.56, f32[768]{0:T(1024)S(1)} %reshape.380, f32[1440]{0:T(1024)S(1)} %fusion.104, f32[1440]{0:T(1024)S(1)} %broadcast_multiply_fusion), kind=kOutput, calls=%fused_computation.50 | convolution fusion | flops 6802661376 | bytes 18007296 | tf_op jit(solution)/shard_map/ti,tj->ij/dot_general | solution.py:185
  653.8 9.8 %reshape.373 = bf16[8,96,4,768]{3,2,1,0:T(4,128)(2,1)} reshape(bf16[768,3072]{1,0:T(8,128)(2,1)} %convolution_convert_fusion.2) | data formatting | bytes 9437184 | tf_op jit(solution)/shard_map/reshape | solution.py:95
  669.0 9.3 %reshape.374 = bf16[32,576,128]{2,1,0:T(8,128)(2,1)} reshape(bf16[8,4,96,768]{3,2,1,0:T(8,128)(2,1)} %bitcast.162) | data formatting | bytes 9437184 | tf_op jit(solution)/shard_map/reshape | solution.py:96
  678.3 9.3 %copy.194 = bf16[8,4,384,192]{3,2,1,0:T(8,128)(2,1)} copy(bf16[8,4,384,192]{2,0,3,1:T(8,128)(2,1)} %bitcast.163) | data formatting | bytes 9437184 | tf_op jit(solution)/shard_map/transpose | solution.py:95
  687.6 12.0 %reshape.376 = bf16[32,576,128]{2,1,0:T(8,128)(2,1)} reshape(bf16[8,4,384,192]{3,2,1,0:T(8,128)(2,1)} %copy.194) | data formatting | bytes 9437184 | tf_op jit(solution)/shard_map/reshape | solution.py:96
  708.4 13.1 %add_convert_fusion.2 = bf16[1440,768]{1,0:T(8,128)(2,1)S(1)} fusion(f32[1440,768]{1,0:T(8,128)} %copy-done.6, bf16[1440,3072]{1,0:T(8,128)(2,1)} %get-tuple-element.75, bf16[3072,768]{0,1:T(8,128)(2,1)} %bitcast.181, f32[768]{0:T(1024)S(1)} %reshape.383), kind=kOutput, calls=%fused_computation.71 | convolution fusion | flops 6798090240 | bytes 20204544 | tf_op jit(solution)/shard_map/dot_general | solution.py:176
  723.6 11.4 %fusion.131 = (f32[768]{0:T(1024)S(1)}, f32[1440]{0:T(1024)S(1)}, f32[1440,768]{1,0:T(8,128)S(1)}) fusion(f32[768]{0:T(1024)S(1)} %copy-done.48, f32[1440]{0:T(1024)S(1)} %copy-done.37, bf16[640,768]{1,0:T(8,128)(2,1)S(1)} %bitcast.172, bf16[800,768]{1,0:T(8,128)(2,1)S(1)} %bitcast.156, bf16[768,2304]{1,0:T(8,128)(2,1)} %reshape.351, ...), kind=kOutput, calls=%fused_computation.185 | convolution fusion | flops 5119301120 | bytes 16827648 | tf_op jit(solution)/shard_map/tj,ij->ti/dot_general | solution.py:210
  749.7 39.8 %psum.7 = f32[9216]{0:T(1024)S(1)} all-reduce(f32[9216]{0:T(1024)S(1)} %constant_dynamic-update-slice_fusion), channel_id=1, replica_groups=mesh['img'=8,'seq'=4] {'img','seq'}, use_global_device_ids=true, to_apply=%region_22.23 | all-reduce | flops 9216 | bytes 73728 | tf_op jit(solution)/shard_map/psum | solution.py:225
  794.7 66.3 %reduce-scatter.5.cloned.1.call-done = bf16[1,1152,128]{2,1,0:T(8,128)(2,1)} async-done(((bf16[32,1152,128]{2,1,0:T(8,128)(2,1)}), bf16[1,1152,128]{2,1,0:T(8,128)(2,1)}) %reduce-scatter.5.cloned.1.call-update) | async-done | bytes 294928 | tf_op jit(solution)/shard_map/reduce_scatter | solution.py:98
  (293 shorter events, 298.7 us)
Async XLA Ops:
  7.2 15.2 %copy-start = (s32[64,40]{0,1:T(8,128)S(1)}, s32[64,40]{0,1:T(8,128)}, u32[]{:S(2)}) copy-start(s32[64,40]{0,1:T(8,128)} %param.21) | copy-start | bytes 30724
  7.2 15.3 %copy-start.10 = (bf16[16,40,768]{2,1,0:T(8,128)(2,1)S(1)}, bf16[16,40,768]{2,1,0:T(8,128)(2,1)}, u32[]{:S(2)}) copy-start(bf16[16,40,768]{2,1,0:T(8,128)(2,1)} %param.19) | copy-start | bytes 2949124
  7.2 15.3 %copy-start.4 = (bf16[4,200,768]{2,1,0:T(8,128)(2,1)S(1)}, bf16[4,200,768]{2,1,0:T(8,128)(2,1)}, u32[]{:S(2)}) copy-start(bf16[4,200,768]{2,1,0:T(8,128)(2,1)} %param.18) | copy-start | bytes 3686404
  7.2 73.8 %all-gather.7.cloned.1.call-start = ((), (), s32[]{:S(2)}) async-start(), calls=%async_computation.4 | async-start | bytes 4325376 | tf_op jit(solution)/shard_map/all_gather | solution.py:76
  16.0 205.4 %all-gather.9.cloned.1.call-start = ((), (), s32[]{:S(2)}) async-start(), calls=%async_computation.5 | async-start | bytes 11354112 | tf_op jit(solution)/shard_map/all_gather | solution.py:76
  22.3 769.2 %reduce-scatter.3.cloned.1.call-start = ((), (), s32[]{:S(2)}) async-start(), calls=%async_computation.2 | async-start | bytes 4866048 | tf_op jit(solution)/shard_map/reduce_scatter | solution.py:98
  23.6 185.4 %copy-start.51 = (pred[4,200]{1,0:T(4,128)(4,1)}, pred[4,200]{1,0:T(4,128)(4,1)S(1)}, u32[]{:S(2)}) copy-start(pred[4,200]{1,0:T(4,128)(4,1)S(1)} %dynamic-slice_compare_fusion) | copy-start | bytes 2404
  23.6 98.3 %copy-start.36 = (f32[1440]{0:T(1024)}, f32[1440]{0:T(1024)S(1)}, u32[]{:S(2)}) copy-start(f32[1440]{0:T(1024)S(1)} %broadcast_multiply_fusion.1) | copy-start | bytes 17284
  25.0 96.9 %copy-start.38 = (f32[1440]{0:T(1024)}, f32[1440]{0:T(1024)S(1)}, u32[]{:S(2)}) copy-start(f32[1440]{0:T(1024)S(1)} %fusion.103) | copy-start | bytes 17284
  84.5 37.5 %copy-start.53 = (f32[768]{0:T(1024)}, f32[768]{0:T(1024)S(1)}, u32[]{:S(2)}) copy-start(f32[768]{0:T(1024)S(1)} %reshape.378) | copy-start | bytes 9220
  84.7 37.3 %copy-start.47 = (f32[768]{0:T(1024)}, f32[768]{0:T(1024)S(1)}, u32[]{:S(2)}) copy-start(f32[768]{0:T(1024)S(1)} %reshape.377) | copy-start | bytes 9220
  136.4 191.7 %copy-start.55 = (f32[768]{0:T(1024)}, f32[768]{0:T(1024)S(1)}, u32[]{:S(2)}) copy-start(f32[768]{0:T(1024)S(1)} %reshape.381) | copy-start | bytes 9220
  324.6 51.7 %slice-start.2 = ((s8[4718592]{0:T(1024)(128)(4,1)}), s8[524288]{0:T(1024)(128)(4,1)S(1)}, s32[]{:S(2)}) async-start(s8[4718592]{0:T(1024)(128)(4,1)} %bitcast.182), calls=%async_computation.8 | async-start | bytes 1048576
  327.4 83.9 %copy-start.6 = (f32[1440,768]{1,0:T(8,128)}, f32[1440,768]{1,0:T(8,128)S(1)}, u32[]{:S(2)}) copy-start(f32[1440,768]{1,0:T(8,128)S(1)} %get-tuple-element.108) | copy-start | bytes 13271044
  328.1 48.2 %copy-start.44 = (f32[1440]{0:T(1024)}, f32[1440]{0:T(1024)S(1)}, u32[]{:S(2)}) copy-start(f32[1440]{0:T(1024)S(1)} %multiply_reduce_fusion.3) | copy-start | bytes 17284
  328.1 48.2 %copy-start.19 = (bf16[4,200,768]{2,1,0:T(8,128)(2,1)S(1)}, bf16[4,200,768]{2,1,0:T(8,128)(2,1)}, u32[]{:S(2)}) copy-start(bf16[4,200,768]{2,1,0:T(8,128)(2,1)} %param.34) | copy-start | bytes 3686404
  328.1 48.2 %slice-start.3 = ((s8[4718592]{0:T(1024)(128)(4,1)}), s8[4194304]{0:T(1024)(128)(4,1)S(1)}, s32[]{:S(2)}) async-start(s8[4718592]{0:T(1024)(128)(4,1)} %bitcast.182), calls=%async_computation.9 | async-start | bytes 8388608
  397.6 13.7 %copy-start.45 = (f32[1440]{0:T(1024)S(1)}, f32[1440]{0:T(1024)}, u32[]{:S(2)}) copy-start(f32[1440]{0:T(1024)} %copy-done.44) | copy-start | bytes 17284
  434.6 10.1 %copy-start.25 = (bf16[16,40,1,12,64]{4,3,2,1,0:T(8,128)(2,1)S(1)}, bf16[16,40,1,12,64]{4,3,2,1,0:T(8,128)(2,1)}, u32[]{:S(2)}) copy-start(bf16[16,40,1,12,64]{4,3,2,1,0:T(8,128)(2,1)} %copy-done.24) | copy-start | bytes 2949124
  475.5 19.7 %copy-start.15 = (bf16[4,200,1,12,64]{1,4,3,0,2:T(8,128)(2,1)S(1)}, bf16[4,200,1,12,64]{1,4,3,0,2:T(8,128)(2,1)}, u32[]{:S(2)}) copy-start(bf16[4,200,1,12,64]{1,4,3,0,2:T(8,128)(2,1)} %copy.213) | copy-start | bytes 3686404
  495.2 19.0 %copy-start.32 = (bf16[768,768]{1,0:T(8,128)(2,1)S(1)}, bf16[768,768]{1,0:T(8,128)(2,1)}, u32[]{:S(2)}) copy-start(bf16[768,768]{1,0:T(8,128)(2,1)} %convolution_convert_fusion.4) | copy-start | bytes 3538948
  541.3 14.1 %copy-start.27 = (bf16[4,200,1,12,64]{1,4,3,0,2:T(8,128)(2,1)S(1)}, bf16[4,200,1,12,64]{1,4,3,0,2:T(8,128)(2,1)}, u32[]{:S(2)}) copy-start(bf16[4,200,1,12,64]{1,4,3,0,2:T(8,128)(2,1)} %fusion.97) | copy-start | bytes 3686404
  564.7 9.8 %copy-start.37 = (f32[1440]{0:T(1024)S(1)}, f32[1440]{0:T(1024)}, u32[]{:S(2)}) copy-start(f32[1440]{0:T(1024)} %copy-done.36) | copy-start | bytes 17284
  564.7 9.8 %copy-start.39 = (f32[1440]{0:T(1024)S(1)}, f32[1440]{0:T(1024)}, u32[]{:S(2)}) copy-start(f32[1440]{0:T(1024)} %copy-done.38) | copy-start | bytes 17284
  564.7 9.8 %copy-start.48 = (f32[768]{0:T(1024)S(1)}, f32[768]{0:T(1024)}, u32[]{:S(2)}) copy-start(f32[768]{0:T(1024)} %copy-done.47) | copy-start | bytes 9220
  564.8 9.8 %copy-start.54 = (f32[768]{0:T(1024)S(1)}, f32[768]{0:T(1024)}, u32[]{:S(2)}) copy-start(f32[768]{0:T(1024)} %copy-done.53) | copy-start | bytes 9220
  613.6 247.5 %reduce-scatter.5.cloned.1.call-start = ((), (), s32[]{:S(2)}) async-start(), calls=%async_computation.3 | async-start | bytes 9732096 | tf_op jit(solution)/shard_map/reduce_scatter | solution.py:98
  708.4 15.2 %copy-start.7 = (bf16[800,2304]{0,1:T(8,128)(2,1)S(1)}, bf16[800,2304]{0,1:T(8,128)(2,1)}, u32[]{:S(2)}) copy-start(bf16[800,2304]{0,1:T(8,128)(2,1)} %convert_element_type.280) | copy-start | bytes 11059204
  722.5 16.6 %slice-start = ((s8[4423680]{0:T(1024)(128)(4,1)}), s8[4194304]{0:T(1024)(128)(4,1)S(1)}, s32[]{:S(2)}) async-start(s8[4423680]{0:T(1024)(128)(4,1)} %bitcast.148), calls=%async_computation.6 | async-start | bytes 8388608
  723.6 11.4 %copy-start.43 = (f32[1440]{0:T(1024)S(1)}, f32[1440]{0:T(1024)}, u32[]{:S(2)}) copy-start(f32[1440]{0:T(1024)} %copy-done.42) | copy-start | bytes 17284
  723.6 15.5 %slice-start.1 = ((s8[4423680]{0:T(1024)(128)(4,1)}), s8[229376]{0:T(1024)(128)(4,1)S(1)}, s32[]{:S(2)}) async-start(s8[4423680]{0:T(1024)(128)(4,1)} %bitcast.148), calls=%async_computation.7 | async-start | bytes 458752
  745.3 118.5 %copy-start.1 = (s32[64,40]{0,1:T(8,128)S(1)}, s32[64,40]{0,1:T(8,128)}, u32[]{:S(2)}) copy-start(s32[64,40]{0,1:T(8,128)} %param.21) | copy-start | bytes 30724
  (35 other events, 149.7 us)
Sparse Core Ops, SparseCore 0:
  16.2 64.7 all-gather.6
  84.4 87.4 all-gather.8
  613.7 105.7 reduce-scatter.2
  726.2 134.7 reduce-scatter.4
where the time goes:
time: 880 us; the launch traced here: 871 us
  local copies, waits for them, and re-layouts  376 us (43%)
  matrix products  256 us (29%)
  waiting for transfers between devices  122 us (14%)
  other arithmetic  62.1 us (7%)
  blocking collectives  39.8 us (5%)
  between operations  14.9 us (2%)
    reduce_scatter x2, waiting for transfers between devices, scatter_mats(): mine = lax.psum_scatter(flat, AXES, scatter_dimension=0, tiled=False)  66.3 us
    all_gather x2, waiting for transfers between devices, gather_mats(): whole = lax.all_gather(flat, AXES, axis=0, tiled=False)  55.9 us
    slice x7, local copies, waits for them, and re-layouts, gather_mats(): piece = whole[:, at:at + rows].reshape((n_img, n_seq) + m.shape)  52.6 us
    dot_general x1, matrix products, body(): jnp.dot(input_two, up_full, preferred_element_type=jnp.float32) + bias_up  48.1 us
    reshape x4, local copies, waits for them, and re-layouts, gather_mats(): piece = whole[:, at:at + rows].reshape((n_img, n_seq) + m.shape)  44.4 us
    psum x1, blocking collectives, body(): vector_sums = lax.psum(jnp.concatenate(vectors), AXES)  39.8 us
    unnamed x144, local copies, waits for them, and re-layouts  36.7 us
    convert_element_type x3, local copies, waits for them, and re-layouts, attend_back(): jnp.stack([grad_query, grad_key, grad_value], axis=2).astype(jnp.bfloat16)  36.6 us
  transfers between devices with their start and end apart: 4, of which 2 were waited for; matrix products, arithmetic and copies ran while one was open for 33% of the time, Pallas kernels for 0%

commit v1 on v0

--- a/solution.py
+++ b/solution.py
@@ -222,7 +222,8 @@
         grad_bias_up,
         grad_bias_down,
     )
-    vector_sums = lax.psum(jnp.concatenate(vectors), AXES)
+    half = lax.psum(jnp.concatenate(vectors), "seq")
+    vector_sums = lax.psum(half, "img")
     vec_out, at = ([], 0)
     for v in vectors:
         width = v.shape[0] // n_seq

time: 880 us -> 880 us (level)
    psum x1 -> x2, blocking collectives: 39.8 us -> 41.8 us  [the longest x1 23.9 us: body(): vector_sums = lax.psum(half, 'img')]
where the time goes in v1:
time: 880 us; the launch traced here: 870 us
  local copies, waits for them, and re-layouts  376 us (43%)
  matrix products  255 us (29%)
  waiting for transfers between devices  120 us (14%)
  other arithmetic  62.1 us (7%)
  blocking collectives  41.8 us (5%)
  between operations  14.9 us (2%)
    reduce_scatter x2, waiting for transfers between devices, scatter_mats(): mine = lax.psum_scatter(flat, AXES, scatter_dimension=0, tiled=False)  64.2 us
    all_gather x2, waiting for transfers between devices, gather_mats(): whole = lax.all_gather(flat, AXES, axis=0, tiled=False)  55.9 us
    slice x7, local copies, waits for them, and re-layouts, gather_mats(): piece = whole[:, at:at + rows].reshape((n_img, n_seq) + m.shape)  52.5 us
    dot_general x1, matrix products, body(): jnp.dot(input_two, up_full, preferred_element_type=jnp.float32) + bias_up  48.1 us
    reshape x4, local copies, waits for them, and re-layouts, gather_mats(): piece = whole[:, at:at + rows].reshape((n_img, n_seq) + m.shape)  44.4 us
    unnamed x144, local copies, waits for them, and re-layouts  36.6 us
    convert_element_type x3, local copies, waits for them, and re-layouts, attend_back(): jnp.stack([grad_query, grad_key, grad_value], axis=2).astype(jnp.bfloat16)  36.6 us
    reshape x6, local copies, waits for them, and re-layouts, scatter_mats(): m.astype(jnp.bfloat16).reshape(n_img, rows, n_seq, cols)  34.1 us
  transfers between devices with their start and end apart: 4, of which 2 were waited for; matrix products, arithmetic and copies ran while one was open for 33% of the time, Pallas kernels for 0%

profile of v1, /device:TPU:0, one launch (start us, length us, event | category | flops | bytes accessed | tf_op | source)
XLA Modules:
  0.0 870.3 jit_solution(5268205859534864148)
XLA Ops:
  25.0 55.9 %all-gather.7.cloned.1.call-done = bf16[32,900,64]{1,2,0:T(8,128)(2,1)} async-done(((bf16[1,900,64]{1,2,0:T(8,128)(2,1)}), bf16[32,900,64]{1,2,0:T(8,128)(2,1)}) %all-gather.7.cloned.1.call-update) | async-done | bytes 3686416 | tf_op jit(solution)/shard_map/all_gather | solution.py:76
  97.2 10.8 %reshape.350 = bf16[8,4,96,576]{3,2,1,0:T(8,128)(2,1)} reshape(bf16[32,864,64]{2,1,0:T(8,128)(2,1)} %copy.143) | data formatting | bytes 7077888 | tf_op jit(solution)/shard_map/reshape | solution.py:80
  122.0 9.1 %fusion.8 = bf16[1440,2304]{1,0:T(8,128)(2,1)S(1)} fusion(bf16[768,2304]{1,0:T(8,128)(2,1)} %reshape.351, f32[2304]{0:T(1024)S(1)} %pad_maximum_fusion.12, f32[768]{0:T(1024)S(1)} %reshape.378, f32[768]{0:T(1024)S(1)} %reshape.377, f32[1440]{0:T(1024)S(1)} %fusion.103, f32[1440]{0:T(1024)S(1)} %broadcast_multiply_fusion.1, ...), kind=kOutput, calls=%fused_computation.22 | convolution fusion | flops 5112668160 | bytes 12413184 | tf_op jit(solution)/shard_map/dot_general | solution.py:163
  136.8 9.8 %reshape_reshape.9 = bf16[16,40,3,12,64]{4,3,2,1,0:T(8,128)(2,1)} reshape(bf16[640,2304]{1,0:T(8,128)(2,1)} %slice.190) | data formatting | bytes 5898240 | tf_op jit(solution)/shard_map/reshape;reshape | solution.py:26
  168.6 12.1 %reshape.398 = bf16[4,200,3,12,64]{4,3,2,1,0:T(8,128)(2,1)} reshape(bf16[800,2304]{1,0:T(8,128)(2,1)} %slice.186) | data formatting | bytes 7372800 | tf_op jit(solution)/shard_map/reshape;reshape | solution.py:26
  240.0 14.1 %fusion.135 = (bf16[32,1152,64]{1,2,0:T(8,128)(2,1)}, bf16[32,1152,64]{1,2,0:T(8,128)(2,1)}) fusion(bf16[32,2592,64]{1,2,0:T(8,128)(2,1)} %all-gather.9.cloned.1.call-done), kind=kLoop, calls=%fused_computation.187 | loop fusion | bytes 18874368 | tf_op jit(solution)/shard_map/slice | solution.py:80
  254.1 9.6 %copy.174 = bf16[32,1152,64]{2,1,0:T(8,128)(2,1)} copy(bf16[32,1152,64]{1,2,0:T(8,128)(2,1)} %get-tuple-element.77) | data formatting | bytes 9437184 | tf_op jit(solution)/shard_map/slice | solution.py:80
  263.7 15.5 %reshape.361 = bf16[8,4,384,192]{3,2,1,0:T(8,128)(2,1)} reshape(bf16[32,1152,64]{2,1,0:T(8,128)(2,1)} %copy.174) | data formatting | bytes 9437184 | tf_op jit(solution)/shard_map/reshape | solution.py:80
  293.6 9.6 %copy.170 = bf16[32,1152,64]{2,1,0:T(8,128)(2,1)} copy(bf16[32,1152,64]{1,2,0:T(8,128)(2,1)} %get-tuple-element.78) | data formatting | bytes 9437184 | tf_op jit(solution)/shard_map/slice | solution.py:80
  303.2 13.3 %reshape.359 = bf16[8,4,96,768]{3,2,1,0:T(8,128)(2,1)} reshape(bf16[32,1152,64]{2,1,0:T(8,128)(2,1)} %copy.170) | data formatting | bytes 9437184 | tf_op jit(solution)/shard_map/reshape | solution.py:80
  328.1 48.1 %multiply_convert_fusion = (bf16[1440,3072]{1,0:T(8,128)(2,1)}, f32[1440,3072]{1,0:T(8,128)}, f32[1440,3072]{1,0:T(8,128)}) fusion(f32[3072]{0:T(1024)S(1)} %reshape.382, bf16[768,3072]{1,0:T(8,128)(2,1)S(1)} %bitcast.185, f32[1440,768]{1,0:T(8,128)S(1)} %get-tuple-element.108, f32[768]{0:T(1024)S(1)} %reshape.381, f32[768]{0:T(1024)S(1)} %reshape.380, ...), kind=kOutput, calls=%fused_computation.6 | convolution fusion | flops 7092264960 | bytes 53409024 | tf_op jit(solution)/shard_map/dot_general | solution.py:173
  376.2 21.3 %convert_reduce_fusion = (f32[3072]{0:T(1024)}, bf16[1440,3072]{1,0:T(8,128)(2,1)}) fusion(f32[1440,3072]{1,0:T(8,128)} %get-tuple-element.76, bf16[3072,768]{0,1:T(8,128)(2,1)S(1)} %bitcast.184, bf16[640,768]{1,0:T(8,128)(2,1)} %bitcast.187, bf16[800,768]{1,0:T(8,128)(2,1)S(1)} %bitcast.177, f32[1440,3072]{1,0:T(8,128)} %get-tuple-element.109, ...), kind=kOutput, calls=%fused_computation.4 | convolution fusion | flops 6874395648 | bytes 51191808 | tf_op jit(solution)/shard_map/tj,ij->ti/dot_general | solution.py:182
  397.5 13.7 %multiply_reduce_fusion.1 = (f32[768]{0:T(1024)}, f32[1440]{0:T(1024)S(1)}, f32[768]{0:T(1024)}, f32[1440,768]{1,0:T(8,128)S(1)}) fusion(f32[1440,768]{1,0:T(8,128)S(1)} %get-tuple-element.108, f32[1440]{0:T(1024)S(1)} %fusion.104, f32[1440]{0:T(1024)S(1)} %broadcast_multiply_fusion, f32[768]{0:T(1024)S(1)} %reshape.380, ...), kind=kOutput, calls=%fused_computation.67 | convolution fusion | flops 6803616768 | bytes 22439808 | tf_op jit(solution)/shard_map/tj,ij->ti/dot_general | solution.py:187
  434.4 10.0 %convert_bitcast_fusion.2 = bf16[16,40,1,12,64]{4,1,3,0,2:T(8,128)(2,1)} fusion(f32[16,12,40,40]{2,3,1,0:T(8,128)} %fusion.100, f32[16,12,40,40]{2,3,1,0:T(8,128)} %copy-done.8, f32[16,12,40]{2,1,0:T(8,128)S(1)} %copy-done.35, bf16[16,40,1,12,64]{4,3,2,1,0:T(8,128)(2,1)} %copy-done.26), kind=kOutput, calls=%fused_computation.98 | convolution fusion | flops 41971240 | bytes 4454400 | tf_op jit(solution)/shard_map/chqk,ckhd->cqhd/dot_general | solution.py:59
  444.5 9.2 %convert_bitcast_fusion.1 = bf16[16,40,1,12,64]{4,1,3,0,2:T(8,128)(2,1)} fusion(f32[16,12,40,40]{2,3,1,0:T(8,128)} %fusion.100, f32[16,12,40,40]{2,3,1,0:T(8,128)} %copy-done.8, f32[16,12,40]{2,1,0:T(8,128)S(1)} %copy-done.35, bf16[16,40,1,12,64]{4,3,2,1,0:T(8,128)(2,1)S(1)} %copy-done.25), kind=kOutput, calls=%fused_computation.97 | convolution fusion | flops 41971240 | bytes 4454400 | tf_op jit(solution)/shard_map/chqk,cqhd->ckhd/dot_general | solution.py:62
  475.4 19.7 %fusion.92 = bf16[4,200,1,12,64]{1,4,3,0,2:T(8,128)(2,1)} fusion(f32[4,12,200,200]{2,3,1,0:T(8,128)} %fusion.81, f32[4,12,200]{2,1,0:T(8,128)S(1)} %copy-done.46, f32[4,12,200,200]{2,3,1,0:T(8,128)} %copy-done.3, pred[4,200]{1,0:T(4,128)(4,1)S(1)} %copy-done.52, bf16[4,200,1,12,64]{1,4,3,0,2:T(8,128)(2,1)S(1)} %copy-done.17), kind=kOutput, calls=%fused_computation.122 | convolution fusion | flops 267504192 | bytes 17856800 | tf_op jit(solution)/shard_map/chqk,ckhd->cqhd/dot_general | solution.py:59
  495.1 19.0 %fusion.87 = bf16[4,200,1,12,64]{1,4,3,0,2:T(8,128)(2,1)} fusion(f32[4,12,200,200]{2,3,1,0:T(8,128)} %fusion.81, f32[4,12,200]{2,1,0:T(8,128)S(1)} %copy-done.46, f32[4,12,200,200]{2,3,1,0:T(8,128)} %copy-done.3, pred[4,200]{1,0:T(4,128)(4,1)S(1)} %copy-done.52, bf16[4,200,1,12,64]{1,4,3,0,2:T(8,128)(2,1)S(1)} %copy-done.15), kind=kOutput, calls=%fused_computation.121 | convolution fusion | flops 267504192 | bytes 17856800 | tf_op jit(solution)/shard_map/chqk,cqhd->ckhd/dot_general | solution.py:62
  528.5 12.8 %copy.203 = bf16[16,40,3,12,64]{1,0,4,3,2:T(8,128)(2,1)} copy(bf16[16,40,3,12,64]{4,1,3,0,2:T(8,128)(2,1)} %pad_maximum_fusion.2) | data formatting | bytes 5898240 | tf_op jit(solution)/shard_map/convert_element_type | solution.py:69
  541.2 14.1 %reshape.397 = bf16[640,2304]{0,1:T(8,128)(2,1)} reshape(bf16[16,40,3,12,64]{1,0,4,3,2:T(8,128)(2,1)} %copy.203) | data formatting | bytes 5898240 | tf_op jit(solution)/shard_map/convert_element_type | solution.py:69
  564.7 9.7 %convert_element_type.280 = bf16[800,2304]{0,1:T(8,128)(2,1)} reshape(bf16[4,200,3,12,64]{1,0,4,3,2:T(4,128)(2,1)} %copy.184) | data formatting | bytes 7372800 | tf_op jit(solution)/shard_map/convert_element_type | solution.py:69
  574.4 12.5 %convolution_convert_fusion = bf16[768,2304]{1,0:T(8,128)(2,1)} fusion(bf16[640,2304]{0,1:T(8,128)(2,1)} %reshape.397, bf16[800,2304]{0,1:T(8,128)(2,1)} %convert_element_type.280, f32[768]{0:T(1024)S(1)} %copy-done.54, f32[768]{0:T(1024)S(1)} %copy-done.48, f32[1440]{0:T(1024)S(1)} %copy-done.39, f32[1440]{0:T(1024)S(1)} %copy-done.37, ...), kind=kOutput, calls=%fused_computation.48 | convolution fusion | flops 5121073152 | bytes 12403968 | tf_op jit(solution)/shard_map/ti,tj->ij/dot_general | solution.py:203
  614.7 12.5 %convolution_convert_fusion.1 = bf16[3072,768]{1,0:T(8,128)(2,1)} fusion(bf16[1440,3072]{1,0:T(8,128)(2,1)} %get-tuple-element.75, bf16[640,768]{1,0:T(8,128)(2,1)} %bitcast.188, bf16[800,768]{1,0:T(8,128)(2,1)S(1)} %bitcast.179), kind=kOutput, calls=%fused_computation.49 | convolution fusion | flops 6801555456 | bytes 15777792 | tf_op jit(solution)/shard_map/ti,tj->ij/dot_general | solution.py:180
  639.5 14.0 %convolution_convert_fusion.2 = bf16[768,3072]{1,0:T(8,128)(2,1)} fusion(bf16[1440,3072]{1,0:T(8,128)(2,1)} %get-tuple-element.113, f32[1440,768]{1,0:T(8,128)} %copy-done.6, f32[768]{0:T(1024)S(1)} %copy-done.56, f32[768]{0:T(1024)S(1)} %reshape.380, f32[1440]{0:T(1024)S(1)} %fusion.104, f32[1440]{0:T(1024)S(1)} %broadcast_multiply_fusion), kind=kOutput, calls=%fused_computation.50 | convolution fusion | flops 6802661376 | bytes 18007296 | tf_op jit(solution)/shard_map/ti,tj->ij/dot_general | solution.py:185
  653.6 9.8 %reshape.373 = bf16[8,96,4,768]{3,2,1,0:T(4,128)(2,1)} reshape(bf16[768,3072]{1,0:T(8,128)(2,1)} %convolution_convert_fusion.2) | data formatting | bytes 9437184 | tf_op jit(solution)/shard_map/reshape | solution.py:95
  668.8 9.3 %reshape.374 = bf16[32,576,128]{2,1,0:T(8,128)(2,1)} reshape(bf16[8,4,96,768]{3,2,1,0:T(8,128)(2,1)} %bitcast.162) | data formatting | bytes 9437184 | tf_op jit(solution)/shard_map/reshape | solution.py:96
  678.1 9.3 %copy.194 = bf16[8,4,384,192]{3,2,1,0:T(8,128)(2,1)} copy(bf16[8,4,384,192]{2,0,3,1:T(8,128)(2,1)} %bitcast.163) | data formatting | bytes 9437184 | tf_op jit(solution)/shard_map/transpose | solution.py:95
  687.3 12.0 %reshape.376 = bf16[32,576,128]{2,1,0:T(8,128)(2,1)} reshape(bf16[8,4,384,192]{3,2,1,0:T(8,128)(2,1)} %copy.194) | data formatting | bytes 9437184 | tf_op jit(solution)/shard_map/reshape | solution.py:96
  708.2 13.1 %add_convert_fusion.2 = bf16[1440,768]{1,0:T(8,128)(2,1)S(1)} fusion(f32[1440,768]{1,0:T(8,128)} %copy-done.6, bf16[1440,3072]{1,0:T(8,128)(2,1)} %get-tuple-element.75, bf16[3072,768]{0,1:T(8,128)(2,1)} %bitcast.181, f32[768]{0:T(1024)S(1)} %reshape.383), kind=kOutput, calls=%fused_computation.71 | convolution fusion | flops 6798090240 | bytes 20204544 | tf_op jit(solution)/shard_map/dot_general | solution.py:176
  723.4 11.4 %fusion.131 = (f32[768]{0:T(1024)S(1)}, f32[1440]{0:T(1024)S(1)}, f32[1440,768]{1,0:T(8,128)S(1)}) fusion(f32[768]{0:T(1024)S(1)} %copy-done.48, f32[1440]{0:T(1024)S(1)} %copy-done.37, bf16[640,768]{1,0:T(8,128)(2,1)S(1)} %bitcast.172, bf16[800,768]{1,0:T(8,128)(2,1)S(1)} %bitcast.156, bf16[768,2304]{1,0:T(8,128)(2,1)} %reshape.351, ...), kind=kOutput, calls=%fused_computation.185 | convolution fusion | flops 5119301120 | bytes 16827648 | tf_op jit(solution)/shard_map/tj,ij->ti/dot_general | solution.py:210
  749.5 18.0 %psum.14 = f32[9216]{0:T(1024)S(1)} all-reduce(f32[9216]{0:T(1024)S(1)} %constant_dynamic-update-slice_fusion), channel_id=1, replica_groups=mesh['img'=8,'seq'=4] {'seq'}, use_global_device_ids=true, to_apply=%region_22.23 | all-reduce | flops 9216 | bytes 73728 | tf_op jit(solution)/shard_map/psum | solution.py:225
  767.4 23.9 %psum.15 = f32[9216]{0:T(1024)S(1)} all-reduce(f32[9216]{0:T(1024)S(1)} %psum.14), channel_id=1, replica_groups=mesh['img'=8,'seq'=4] {'img'}, use_global_device_ids=true, to_apply=%region_23.24 | all-reduce | flops 9216 | bytes 73728 | tf_op jit(solution)/shard_map/psum | solution.py:226
  796.5 64.2 %reduce-scatter.5.cloned.1.call-done = bf16[1,1152,128]{2,1,0:T(8,128)(2,1)} async-done(((bf16[32,1152,128]{2,1,0:T(8,128)(2,1)}), bf16[1,1152,128]{2,1,0:T(8,128)(2,1)}) %reduce-scatter.5.cloned.1.call-update) | async-done | bytes 294928 | tf_op jit(solution)/shard_map/reduce_scatter | solution.py:98
  (294 shorter events, 307.7 us)
Async XLA Ops:
  7.2 15.2 %copy-start = (s32[64,40]{0,1:T(8,128)S(1)}, s32[64,40]{0,1:T(8,128)}, u32[]{:S(2)}) copy-start(s32[64,40]{0,1:T(8,128)} %param.21) | copy-start | bytes 30724
  7.2 15.3 %copy-start.10 = (bf16[16,40,768]{2,1,0:T(8,128)(2,1)S(1)}, bf16[16,40,768]{2,1,0:T(8,128)(2,1)}, u32[]{:S(2)}) copy-start(bf16[16,40,768]{2,1,0:T(8,128)(2,1)} %param.19) | copy-start | bytes 2949124
  7.2 15.3 %copy-start.4 = (bf16[4,200,768]{2,1,0:T(8,128)(2,1)S(1)}, bf16[4,200,768]{2,1,0:T(8,128)(2,1)}, u32[]{:S(2)}) copy-start(bf16[4,200,768]{2,1,0:T(8,128)(2,1)} %param.18) | copy-start | bytes 3686404
  7.2 73.8 %all-gather.7.cloned.1.call-start = ((), (), s32[]{:S(2)}) async-start(), calls=%async_computation.4 | async-start | bytes 4325376 | tf_op jit(solution)/shard_map/all_gather | solution.py:76
  16.0 205.5 %all-gather.9.cloned.1.call-start = ((), (), s32[]{:S(2)}) async-start(), calls=%async_computation.5 | async-start | bytes 11354112 | tf_op jit(solution)/shard_map/all_gather | solution.py:76
  22.3 771.0 %reduce-scatter.3.cloned.1.call-start = ((), (), s32[]{:S(2)}) async-start(), calls=%async_computation.2 | async-start | bytes 4866048 | tf_op jit(solution)/shard_map/reduce_scatter | solution.py:98
  23.6 185.5 %copy-start.51 = (pred[4,200]{1,0:T(4,128)(4,1)}, pred[4,200]{1,0:T(4,128)(4,1)S(1)}, u32[]{:S(2)}) copy-start(pred[4,200]{1,0:T(4,128)(4,1)S(1)} %dynamic-slice_compare_fusion) | copy-start | bytes 2404
  23.6 98.3 %copy-start.36 = (f32[1440]{0:T(1024)}, f32[1440]{0:T(1024)S(1)}, u32[]{:S(2)}) copy-start(f32[1440]{0:T(1024)S(1)} %broadcast_multiply_fusion.1) | copy-start | bytes 17284
  25.0 96.9 %copy-start.38 = (f32[1440]{0:T(1024)}, f32[1440]{0:T(1024)S(1)}, u32[]{:S(2)}) copy-start(f32[1440]{0:T(1024)S(1)} %fusion.103) | copy-start | bytes 17284
  84.5 37.5 %copy-start.53 = (f32[768]{0:T(1024)}, f32[768]{0:T(1024)S(1)}, u32[]{:S(2)}) copy-start(f32[768]{0:T(1024)S(1)} %reshape.378) | copy-start | bytes 9220
  84.7 37.3 %copy-start.47 = (f32[768]{0:T(1024)}, f32[768]{0:T(1024)S(1)}, u32[]{:S(2)}) copy-start(f32[768]{0:T(1024)S(1)} %reshape.377) | copy-start | bytes 9220
  136.4 191.6 %copy-start.55 = (f32[768]{0:T(1024)}, f32[768]{0:T(1024)S(1)}, u32[]{:S(2)}) copy-start(f32[768]{0:T(1024)S(1)} %reshape.381) | copy-start | bytes 9220
  324.5 51.7 %slice-start.2 = ((s8[4718592]{0:T(1024)(128)(4,1)}), s8[524288]{0:T(1024)(128)(4,1)S(1)}, s32[]{:S(2)}) async-start(s8[4718592]{0:T(1024)(128)(4,1)} %bitcast.182), calls=%async_computation.8 | async-start | bytes 1048576
  327.3 83.9 %copy-start.6 = (f32[1440,768]{1,0:T(8,128)}, f32[1440,768]{1,0:T(8,128)S(1)}, u32[]{:S(2)}) copy-start(f32[1440,768]{1,0:T(8,128)S(1)} %get-tuple-element.108) | copy-start | bytes 13271044
  328.0 48.2 %copy-start.44 = (f32[1440]{0:T(1024)}, f32[1440]{0:T(1024)S(1)}, u32[]{:S(2)}) copy-start(f32[1440]{0:T(1024)S(1)} %multiply_reduce_fusion.3) | copy-start | bytes 17284
  328.0 48.2 %copy-start.19 = (bf16[4,200,768]{2,1,0:T(8,128)(2,1)S(1)}, bf16[4,200,768]{2,1,0:T(8,128)(2,1)}, u32[]{:S(2)}) copy-start(bf16[4,200,768]{2,1,0:T(8,128)(2,1)} %param.34) | copy-start | bytes 3686404
  328.0 48.1 %slice-start.3 = ((s8[4718592]{0:T(1024)(128)(4,1)}), s8[4194304]{0:T(1024)(128)(4,1)S(1)}, s32[]{:S(2)}) async-start(s8[4718592]{0:T(1024)(128)(4,1)} %bitcast.182), calls=%async_computation.9 | async-start | bytes 8388608
  397.5 13.7 %copy-start.45 = (f32[1440]{0:T(1024)S(1)}, f32[1440]{0:T(1024)}, u32[]{:S(2)}) copy-start(f32[1440]{0:T(1024)} %copy-done.44) | copy-start | bytes 17284
  434.4 10.0 %copy-start.25 = (bf16[16,40,1,12,64]{4,3,2,1,0:T(8,128)(2,1)S(1)}, bf16[16,40,1,12,64]{4,3,2,1,0:T(8,128)(2,1)}, u32[]{:S(2)}) copy-start(bf16[16,40,1,12,64]{4,3,2,1,0:T(8,128)(2,1)} %copy-done.24) | copy-start | bytes 2949124
  475.4 19.7 %copy-start.15 = (bf16[4,200,1,12,64]{1,4,3,0,2:T(8,128)(2,1)S(1)}, bf16[4,200,1,12,64]{1,4,3,0,2:T(8,128)(2,1)}, u32[]{:S(2)}) copy-start(bf16[4,200,1,12,64]{1,4,3,0,2:T(8,128)(2,1)} %copy.213) | copy-start | bytes 3686404
  495.1 19.0 %copy-start.32 = (bf16[768,768]{1,0:T(8,128)(2,1)S(1)}, bf16[768,768]{1,0:T(8,128)(2,1)}, u32[]{:S(2)}) copy-start(bf16[768,768]{1,0:T(8,128)(2,1)} %convolution_convert_fusion.4) | copy-start | bytes 3538948
  541.2 14.1 %copy-start.27 = (bf16[4,200,1,12,64]{1,4,3,0,2:T(8,128)(2,1)S(1)}, bf16[4,200,1,12,64]{1,4,3,0,2:T(8,128)(2,1)}, u32[]{:S(2)}) copy-start(bf16[4,200,1,12,64]{1,4,3,0,2:T(8,128)(2,1)} %fusion.97) | copy-start | bytes 3686404
  564.6 9.8 %copy-start.37 = (f32[1440]{0:T(1024)S(1)}, f32[1440]{0:T(1024)}, u32[]{:S(2)}) copy-start(f32[1440]{0:T(1024)} %copy-done.36) | copy-start | bytes 17284
  564.6 9.8 %copy-start.39 = (f32[1440]{0:T(1024)S(1)}, f32[1440]{0:T(1024)}, u32[]{:S(2)}) copy-start(f32[1440]{0:T(1024)} %copy-done.38) | copy-start | bytes 17284
  564.6 9.8 %copy-start.48 = (f32[768]{0:T(1024)S(1)}, f32[768]{0:T(1024)}, u32[]{:S(2)}) copy-start(f32[768]{0:T(1024)} %copy-done.47) | copy-start | bytes 9220
  564.6 9.8 %copy-start.54 = (f32[768]{0:T(1024)S(1)}, f32[768]{0:T(1024)}, u32[]{:S(2)}) copy-start(f32[768]{0:T(1024)} %copy-done.53) | copy-start | bytes 9220
  613.4 247.3 %reduce-scatter.5.cloned.1.call-start = ((), (), s32[]{:S(2)}) async-start(), calls=%async_computation.3 | async-start | bytes 9732096 | tf_op jit(solution)/shard_map/reduce_scatter | solution.py:98
  708.2 15.2 %copy-start.7 = (bf16[800,2304]{0,1:T(8,128)(2,1)S(1)}, bf16[800,2304]{0,1:T(8,128)(2,1)}, u32[]{:S(2)}) copy-start(bf16[800,2304]{0,1:T(8,128)(2,1)} %convert_element_type.280) | copy-start | bytes 11059204
  722.3 16.6 %slice-start = ((s8[4423680]{0:T(1024)(128)(4,1)}), s8[4194304]{0:T(1024)(128)(4,1)S(1)}, s32[]{:S(2)}) async-start(s8[4423680]{0:T(1024)(128)(4,1)} %bitcast.148), calls=%async_computation.6 | async-start | bytes 8388608
  723.4 11.4 %copy-start.43 = (f32[1440]{0:T(1024)S(1)}, f32[1440]{0:T(1024)}, u32[]{:S(2)}) copy-start(f32[1440]{0:T(1024)} %copy-done.42) | copy-start | bytes 17284
  723.4 15.5 %slice-start.1 = ((s8[4423680]{0:T(1024)(128)(4,1)}), s8[229376]{0:T(1024)(128)(4,1)S(1)}, s32[]{:S(2)}) async-start(s8[4423680]{0:T(1024)(128)(4,1)} %bitcast.148), calls=%async_computation.7 | async-start | bytes 458752
  745.1 118.4 %copy-start.1 = (s32[64,40]{0,1:T(8,128)S(1)}, s32[64,40]{0,1:T(8,128)}, u32[]{:S(2)}) copy-start(s32[64,40]{0,1:T(8,128)} %param.21) | copy-start | bytes 30724
  (35 other events, 149.7 us)
Sparse Core Ops, SparseCore 0:
  16.2 64.7 all-gather.6
  84.4 87.4 all-gather.8
  613.5 105.6 reduce-scatter.2
  726.0 134.6 reduce-scatter.4
